TPU v7x, 256 devices: a whole 4x4x8 slice. The times are simulated.
256 devices in a mesh: req: 32 (over y, z_hi, core), tp: 8 (over z_lo, x).
Axes of the slice: x: 4, y: 4, z: 8 (z_hi: 4, z_lo: 2; z = z_hi * 2 + z_lo), core: 2. Of those that a mesh axis runs over, the one named last changes fastest.
Arguments:
- tokens: bfloat16 [16384, 2048], P(('req', 'tp')), may hold values from -40 to 40, as said below
- attn_gain: float32 [2048], replicated, may hold values from 0.25 to 1.75
- w_query: bfloat16 [2048, 2048], P(None, 'tp'), may hold values from -0.125 to 0.125
- key_weight: bfloat16 [2048, 1024], P(None, 'tp'), may hold values from -0.125 to 0.125
- value_weight: bfloat16 [2048, 1024], P(None, 'tp'), may hold values from -0.125 to 0.125
- w_headgate: bfloat16 [2048, 16], P(None, 'tp'), may hold values from -0.125 to 0.125
- query_gain: float32 [128], replicated, may hold values from 1.3 to 2
- key_gain: float32 [128], replicated, may hold values from 1.3 to 2
- w_out: bfloat16 [2048, 2048], P('tp'), may hold values from -0.5 to 0.5
- mlp_gain: float32 [2048], replicated, may hold values from 0.25 to 1.75
- w_gate: bfloat16 [2048, 3072], P(None, 'tp'), may hold values from -0.125 to 0.125
- w_up: bfloat16 [2048, 3072], P(None, 'tp'), may hold values from -0.125 to 0.125
- w_down: bfloat16 [3072, 2048], P('tp'), may hold values from -0.109375 to 0.109375
- pooled_keys: bfloat16 [16384, 16, 8, 128], P(('req', 'tp')), may hold values from -150 to 150, as said below
- pooled_values: bfloat16 [16384, 16, 8, 128], P(('req', 'tp')), may hold values from -6 to 6
- sink_key_cache: bfloat16 [64, 4, 8, 128], P('req', None, 'tp'), may hold values from -12 to 12
- sink_value_cache: bfloat16 [64, 4, 8, 128], P('req', None, 'tp'), may hold values from -6 to 6
- cached_length: int32 [64], P('req'), may hold values from 0 to 32768, as said below
- valid_length: int32 [64], P('req'), may hold values from 1 to 256, as said below
- sink_position_count: int32 [64], P('req'), may hold values from 0 to 4, as said below
- window: int32 [64], P('req'), may hold values from 2048 to 4096, as said below
- page_slot: int32 [32, 512], P('req'), may hold values from 0 to 511, each once within a row
Outputs:
- out: float32 [16384, 2048], P(('req', 'tp'))
- app_keys: bfloat16 [16384, 8, 128], P('req', 'tp')
- app_values: bfloat16 [16384, 8, 128], P('req', 'tp')
Inputs may be any that keep to these rules, and one draw needn't show every extreme that they name: `tokens`: rows of the input; rows and features have unlike scales. `pooled_keys`: keys as the cache stores them. `cached_length`: short requests lie below 4096; some request has exactly 32768. `valid_length`: the rest of a span is padding; some request has exactly 256. `sink_position_count`: some request has exactly 4. `window`: some request has exactly 4096. `page_slot`: each row is a permutation.
All inputs are finite; a program needn't handle non-finite values.
Results may differ from a plain program's by a relative error of at most 0.02.
The roundings to bfloat16 on the way count: a program that leaves them out, or rounds other values in their place, can miss the bound.
Values may be sent and summed in bfloat16 or wider, within the bound.
A program may use at most 128 MiB of HBM per device.

v0:
```python
import math
import jax
import jax.numpy as jnp
from jax import lax
from jax.sharding import PartitionSpec as P

WINDOW_TOKENS = 4096
SPAN_TOKENS = 256
EPSILON = 1e-06
ROPE_BASE = 1000000.0
NEG_FILL = -1e30


def rms_rows(values, gain):
    mean_square = jnp.mean(values * values, axis=-1, keepdims=True)
    return values * lax.rsqrt(mean_square + EPSILON) * gain


def rotary(heads, positions):
    head_width = heads.shape[-1]
    half_width = head_width // 2
    freqs = ROPE_BASE ** (-2.0 * jnp.arange(half_width, dtype=jnp.float32) / head_width)
    angles = positions.astype(jnp.float32)[:, None] * freqs[None, :]
    cosine = jnp.cos(angles)[:, None, :]
    sine_part = jnp.sin(angles)[:, None, :]
    first_half = heads[..., :half_width]
    second_half = heads[..., half_width:]
    return jnp.concatenate(
        [
            first_half * cosine - second_half * sine_part,
            second_half * cosine + first_half * sine_part,
        ],
        axis=-1,
    )


def swiglu(normed_rows, w_gate, w_up):
    gate_part = jnp.dot(normed_rows, w_gate, preferred_element_type=jnp.float32)
    up_part = jnp.dot(normed_rows, w_up, preferred_element_type=jnp.float32)
    return (jax.nn.silu(gate_part) * up_part).astype(jnp.bfloat16)


def masked_max(scores, allowed):
    return jnp.max(jnp.where(allowed, scores, NEG_FILL), axis=-1)


def near_masks(cached, valid, sinks_used, reach, span_len, window_len, sink_len):
    offsets = jnp.arange(span_len, dtype=jnp.int32)
    sink_slots = jnp.arange(sink_len, dtype=jnp.int32)
    sink_ok = (sink_slots[None, :] < sinks_used[:, None]) & (
        sink_slots[None, :] < (cached - window_len)[:, None]
    )
    span_ok = (
        (offsets[None, None, :] < valid[:, None, None])
        & (offsets[None, None, :] <= offsets[None, :, None])
        & (
            (cached[:, None, None] + offsets[None, None, :] < sinks_used[:, None, None])
            | (offsets[None, :, None] - offsets[None, None, :] <= reach[:, None, None])
        )
    )
    return (sink_ok[:, None, None, None, :], span_ok[:, :, None, None, :])


def near_scores(query_vectors, sink_key_rows, fresh_keys, score_scale):
    sink_scores = (
        jnp.einsum(
            "rckgd,rskd->rckgs", query_vectors, sink_key_rows, preferred_element_type=jnp.float32
        )
        * score_scale
    )
    span_scores = (
        jnp.einsum(
            "rckgd,rtkd->rckgt", query_vectors, fresh_keys, preferred_element_type=jnp.float32
        )
        * score_scale
    )
    return (sink_scores, span_scores)


def attend_whole(
    query_vectors,
    sink_key_rows,
    sink_value_rows,
    window_key_rows,
    window_value_rows,
    fresh_keys,
    fresh_values,
    cached,
    valid,
    sinks_used,
    reach,
    score_scale,
):
    span_len = query_vectors.shape[1]
    window_len = window_key_rows.shape[1]
    sink_ok, span_ok = near_masks(
        cached, valid, sinks_used, reach, span_len, window_len, sink_key_rows.shape[1]
    )
    offsets = jnp.arange(span_len, dtype=jnp.int32)
    window_slots = jnp.arange(window_len, dtype=jnp.int32)
    key_positions = cached[:, None] - window_len + window_slots[None, :]
    window_ok = (key_positions[:, None, :] >= 0) & (
        (key_positions[:, None, :] < sinks_used[:, None, None])
        | (
            (window_len - window_slots)[None, None, :] + offsets[None, :, None]
            <= reach[:, None, None]
        )
    )
    window_ok = window_ok[:, :, None, None, :]
    sink_scores, span_scores = near_scores(query_vectors, sink_key_rows, fresh_keys, score_scale)
    window_scores = (
        jnp.einsum(
            "rckgd,rwkd->rckgw", query_vectors, window_key_rows, preferred_element_type=jnp.float32
        )
        * score_scale
    )
    highest = jnp.maximum(
        jnp.maximum(masked_max(sink_scores, sink_ok), masked_max(window_scores, window_ok)),
        masked_max(span_scores, span_ok),
    )[..., None]
    sink_weights = jnp.where(sink_ok, jnp.exp(sink_scores - highest), 0.0)
    window_weights = jnp.where(window_ok, jnp.exp(window_scores - highest), 0.0)
    span_weights = jnp.where(span_ok, jnp.exp(span_scores - highest), 0.0)
    total = (
        jnp.sum(sink_weights, axis=-1)
        + jnp.sum(window_weights, axis=-1)
        + jnp.sum(span_weights, axis=-1)
    )
    summed = jnp.einsum(
        "rckgs,rskd->rckgd",
        sink_weights.astype(jnp.bfloat16),
        sink_value_rows,
        preferred_element_type=jnp.float32,
    )
    summed = summed + jnp.einsum(
        "rckgw,rwkd->rckgd",
        window_weights.astype(jnp.bfloat16),
        window_value_rows,
        preferred_element_type=jnp.float32,
    )
    summed = summed + jnp.einsum(
        "rckgt,rtkd->rckgd",
        span_weights.astype(jnp.bfloat16),
        fresh_values,
        preferred_element_type=jnp.float32,
    )
    return summed / total[..., None]


def body(
    tokens,
    attn_gain,
    w_query,
    key_weight,
    value_weight,
    w_headgate,
    query_gain,
    key_gain,
    w_out,
    mlp_gain,
    w_gate,
    w_up,
    w_down,
    pooled_keys,
    pooled_values,
    sink_key_cache,
    sink_value_cache,
    cached_length,
    valid_length,
    sink_position_count,
    window,
    page_slot,
):
    head_dim = query_gain.shape[0]
    heads_dev = w_query.shape[1] // head_dim
    kv_dev = key_weight.shape[1] // head_dim
    group_size = heads_dev // kv_dev
    requests_dev = cached_length.shape[0]
    window_len = WINDOW_TOKENS
    span_len = SPAN_TOKENS
    rows_own = tokens.shape[0]
    score_scale = 1.0 / math.sqrt(head_dim)
    tp_index = lax.axis_index("tp")
    all_rows = lax.all_gather(tokens, "tp", axis=0, tiled=True)
    residual = all_rows.astype(jnp.float32)
    normalized_input = rms_rows(residual, attn_gain).astype(jnp.bfloat16)
    rows_total = normalized_input.shape[0]
    offsets = jnp.arange(span_len, dtype=jnp.int32)
    positions = (cached_length[:, None] + offsets[None, :]).reshape(rows_total)
    query_vectors = jnp.dot(normalized_input, w_query, preferred_element_type=jnp.float32).reshape(
        rows_total, heads_dev, head_dim
    )
    query_vectors = rotary(rms_rows(query_vectors, query_gain), positions).astype(jnp.bfloat16)
    fresh_keys = jnp.dot(normalized_input, key_weight, preferred_element_type=jnp.float32).reshape(
        rows_total, kv_dev, head_dim
    )
    fresh_keys = rotary(rms_rows(fresh_keys, key_gain), positions).astype(jnp.bfloat16)
    fresh_values = (
        jnp.dot(normalized_input, value_weight, preferred_element_type=jnp.float32)
        .astype(jnp.bfloat16)
        .reshape(rows_total, kv_dev, head_dim)
    )
    headgate = jax.nn.sigmoid(
        jnp.dot(normalized_input, w_headgate, preferred_element_type=jnp.float32)
    )
    present = (offsets[None, :] < valid_length[:, None]).reshape(rows_total)[:, None, None]
    app_keys = jnp.where(present, fresh_keys, jnp.zeros_like(fresh_keys))
    app_values = jnp.where(present, fresh_values, jnp.zeros_like(fresh_values))
    query_blocks = query_vectors.reshape(requests_dev, span_len, kv_dev, group_size, head_dim)
    key_blocks = fresh_keys.reshape(requests_dev, span_len, kv_dev, head_dim)
    value_blocks = fresh_values.reshape(requests_dev, span_len, kv_dev, head_dim)
    arrived_keys, arrived_values = (
        lax.all_to_all(pooled_keys, "tp", split_axis=2, concat_axis=0, tiled=True),
        lax.all_to_all(pooled_values, "tp", split_axis=2, concat_axis=0, tiled=True),
    )
    window_key_rows = jnp.take(arrived_keys, page_slot[0], axis=0).reshape(
        requests_dev, window_len, kv_dev, head_dim
    )
    window_value_rows = jnp.take(arrived_values, page_slot[0], axis=0).reshape(
        requests_dev, window_len, kv_dev, head_dim
    )
    mixture = attend_whole(
        query_blocks,
        sink_key_cache,
        sink_value_cache,
        window_key_rows,
        window_value_rows,
        key_blocks,
        value_blocks,
        cached_length,
        valid_length,
        sink_position_count,
        window,
        score_scale,
    )
    mixture = mixture.reshape(rows_total, heads_dev, head_dim)
    heads_out = (
        (mixture * headgate[..., None])
        .astype(jnp.bfloat16)
        .reshape(rows_total, heads_dev * head_dim)
    )
    attn = lax.psum(
        jnp.dot(heads_out, w_out, preferred_element_type=jnp.float32).astype(jnp.bfloat16), "tp"
    ).astype(jnp.float32)
    middle = residual + attn
    hidden = swiglu(rms_rows(middle, mlp_gain).astype(jnp.bfloat16), w_gate, w_up)
    branch = lax.psum(
        jnp.dot(hidden, w_down, preferred_element_type=jnp.float32).astype(jnp.bfloat16), "tp"
    ).astype(jnp.float32)
    row_start = tp_index * rows_own
    output = lax.dynamic_slice_in_dim(middle, row_start, rows_own, 0) + lax.dynamic_slice_in_dim(
        branch, row_start, rows_own, 0
    )
    return (output, app_keys, app_values)


def solution(mesh):
    in_specs = (
        P(("req", "tp"), None),
        P(),
        P(None, "tp"),
        P(None, "tp"),
        P(None, "tp"),
        P(None, "tp"),
        P(),
        P(),
        P("tp", None),
        P(),
        P(None, "tp"),
        P(None, "tp"),
        P("tp", None),
        P(("req", "tp"), None, None, None),
        P(("req", "tp"), None, None, None),
        P("req", None, "tp", None),
        P("req", None, "tp", None),
        P("req"),
        P("req"),
        P("req"),
        P("req"),
        P("req", None),
    )
    out_specs = (P(("req", "tp"), None), P("req", "tp", None), P("req", "tp", None))
    return jax.shard_map(body, mesh=mesh, in_specs=in_specs, out_specs=out_specs, check_vma=False)
```

profile of v0, /device:TPU:8, one launch (start us, length us, event | category | flops | bytes accessed | tf_op | source)
XLA Modules:
  0.0 337.1 jit_solution(11308946592861896893)
XLA Ops:
  7.2 0.7 all-gather.2.cloned.1.call-update
  7.9 3.2 copy.39
  11.1 5.8 %all-to-all-start.1 = ((bf16[64,16,8,128]{3,1,0,2:T(8,128)(2,1)}), bf16[64,16,8,128]{3,1,0,2:T(8,128)(2,1)}, u32[]{:S(2)}, u32[]{:S(2)}) async-start(bf16[64,16,8,128]{3,1,0,2:T(8,128)(2,1)} %copy.39), calls=%async_computation.1 | async-start | bytes 4194304 | tf_op jit(solution)/shard_map/all_to_all | solution.py:214
  17.2 3.2 copy.36
  20.5 0.5 multiply_cosine_fusion.1
  21.0 0.2 or_and_fusion.1
  21.3 0.6 iota_add_fusion
  22.0 4.6 %or_and_fusion = pred[2,256,4096]{1,2,0:T(8,128)(4,1)} fusion(s32[256,4096]{0,1:T(8,128)S(1)} %iota_add_fusion, s32[2]{0:T(128)S(1)} %copy-done.16, pred[2,4096]{1,0:T(4,128)(4,1)S(1)} %get-tuple-element.21, pred[2,4096]{1,0:T(4,128)(4,1)S(1)} %get-tuple-element.20), kind=kLoop, calls=%fused_computation.12 | loop fusion | flops 6291456 | bytes 6307848 | tf_op jit(solution)/shard_map/and | solution.py:102
  26.5 22.6 %all-to-all-done.1 = bf16[64,16,8,128]{3,1,0,2:T(8,128)(2,1)} async-done(((bf16[64,16,8,128]{3,1,0,2:T(8,128)(2,1)}), bf16[64,16,8,128]{3,1,0,2:T(8,128)(2,1)}, u32[]{:S(2)}, u32[]{:S(2)}) %all-to-all-start.1) | async-done | bytes 2097184 | tf_op jit(solution)/shard_map/all_to_all | solution.py:214
  49.1 5.7 %all-to-all-start = ((bf16[64,16,8,128]{3,1,0,2:T(8,128)(2,1)}), bf16[64,16,8,128]{3,1,0,2:T(8,128)(2,1)}, u32[]{:S(2)}, u32[]{:S(2)}) async-start(bf16[64,16,8,128]{3,1,0,2:T(8,128)(2,1)} %copy.36), calls=%async_computation | async-start | bytes 4194304 | tf_op jit(solution)/shard_map/all_to_all | solution.py:213
  54.9 30.4 %all-gather.2.cloned.1.call-done = bf16[512,2048]{1,0:T(8,128)(2,1)} async-done(((bf16[64,2048]{1,0:T(8,128)(2,1)}), bf16[512,2048]{1,0:T(8,128)(2,1)}) %all-gather.2.cloned.1.call-update) | async-done | bytes 2097168 | tf_op jit(solution)/shard_map/all_gather | solution.py:184
  85.4 2.2 fusion.9
  87.6 0.5 fusion.11
  88.2 1.4 copy-done.1
  89.5 0.7 fusion.20
  90.2 0.1 copy.47
  90.4 2.6 multiply_reduce_fusion.1
  93.3 0.2 copy.35
  93.5 0.2 copy.34
  93.7 0.3 copy-done.8
  94.1 2.4 multiply_reduce_fusion.2
  96.6 0.6 fusion.44
  97.3 0.1 copy.59
  97.4 4.0 %gather_fusion.1 = bf16[512,16,128]{2,1,0:T(8,128)(2,1)} fusion(bf16[512,16,128]{2,1,0:T(8,128)(2,1)} %bitcast.34, s32[1024]{0:T(1024)S(1)} %pad_clamp_fusion), kind=kCustom, calls=%fused_computation.1.clone | custom fusion | bytes 4196352 | tf_op jit(solution)/shard_map/jit(_take)/gather | solution.py:219
  101.5 2.3 convolution_convert_fusion.2
  103.8 4.0 %gather_fusion = bf16[512,16,128]{2,1,0:T(8,128)(2,1)} fusion(bf16[512,16,128]{2,1,0:T(8,128)(2,1)} %bitcast.11, s32[1024]{0:T(1024)S(1)} %pad_clamp_fusion), kind=kCustom, calls=%fused_computation.clone | custom fusion | bytes 4196352 | tf_op jit(solution)/shard_map/jit(_take)/gather | solution.py:216
  107.8 4.9 %bitcast_select_fusion.1 = (bf16[512,16,1,128]{3,1,0,2:T(8,128)(2,1)}, bf16[512,16,1,128]{3,1,0,2:T(8,128)(2,1)}) fusion(bf16[512,16,128]{2,1,0:T(8,128)(2,1)} %gather_fusion.1, pred[512]{0:T(512)(128)(4,1)S(1)} %compare_and_fusion, bf16[512,16,128]{2,1,0:T(8,128)(2,1)} %gather_fusion), kind=kLoop, calls=%fused_computation.24 | loop fusion | flops 2097152 | bytes 8389120 | tf_op jit(solution)/shard_map/jit(_take)/select_n | solution.py:219
  112.7 0.3 select_reduce_fusion.1
  112.9 4.1 %fusion = (f32[2,256,2]{1,2,0:T(2,128)S(1)}, f32[2,4096,256,2]{2,1,3,0:T(8,128)S(1)}) fusion(pred[2,256,4096]{1,2,0:T(8,128)(4,1)S(1)} %copy-done.5, bf16[2,4096,128,1]{2,1,3,0:T(8,128)(2,1)} %bitcast.160, bf16[2,256,2,64]{3,1,2,0:T(8,128)(2,1)S(1)} %copy.35, bf16[2,256,2,64]{3,1,2,0:T(8,128)(2,1)S(1)} %copy.34), kind=kOutput, calls=%fused_computation.4 | convolution fusion | flops 1086848000 | bytes 21237760 | tf_op jit(solution)/shard_map/rckgd,rwkd->rckgw/dot_general | solution.py:112
  117.0 0.4 select_reduce_fusion
  117.5 0.2 fusion.23
  117.7 0.4 fusion.31
  118.1 3.9 %fusion.3 = f32[2,256,2]{1,2,0:T(2,128)S(1)} fusion(f32[2,4096,256,2]{2,1,3,0:T(8,128)S(1)} %get-tuple-element.31, f32[2,256,2]{1,2,0:T(2,128)S(1)} %maximum_maximum_fusion, pred[2,256,4096]{1,2,0:T(8,128)(4,1)S(1)} %copy-done.5), kind=kLoop, calls=%fused_computation.7 | loop fusion | flops 16776192 | bytes 18882560 | tf_op jit(solution)/shard_map/reduce_sum | solution.py:126
  122.1 0.7 copy-done.4
  122.8 9.7 %fusion.6 = f32[2,128,256,2]{1,2,3,0:T(8,128)S(1)} fusion(bf16[2,4096,128,1]{2,1,3,0:T(8,128)(2,1)} %bitcast.159, f32[2,4096,256,2]{2,1,3,0:T(8,128)} %copy-done.4, f32[2,256,2]{1,2,0:T(2,128)S(1)} %maximum_maximum_fusion, pred[2,256,4096]{1,2,0:T(8,128)(4,1)} %or_and_fusion), kind=kOutput, calls=%fused_computation.10 | convolution fusion | flops 1090519040 | bytes 21499904 | tf_op jit(solution)/shard_map/rckgw,rwkd->rckgd/dot_general | solution.py:135
  132.6 0.4 fusion.22
  133.0 0.4 copy.46
  133.4 0.6 mul.265
  134.0 2.0 convolution_convert_fusion
  136.1 0.3 all-reduce.5.cloned.1.call-start
  136.4 90.3 %all-reduce.3.cloned.1.call-done = bf16[512,2048]{1,0:T(8,128)(2,1)} async-done(((bf16[512,2048]{1,0:T(8,128)(2,1)}), bf16[512,2048]{1,0:T(8,128)(2,1)}) %all-reduce.3.cloned.1.call-update) | async-done | bytes 2097168 | tf_op jit(solution)/shard_map/psum | solution.py:242
  226.6 5.0 %multiply_reduce_fusion = (f32[512]{0:T(512)S(1)}, f32[512,2048]{1,0:T(8,128)}) fusion(bf16[512,2048]{1,0:T(8,128)(2,1)} %all-reduce.3.cloned.1.call-done, bf16[512,2048]{1,0:T(8,128)(2,1)} %all-gather.2.cloned.1.call-done), kind=kLoop, calls=%fused_computation.20 | loop fusion | flops 5242368 | bytes 8390656 | tf_op jit(solution)/shard_map/reduce_sum | solution.py:15
  231.7 2.7 fusion.66
  234.4 6.4 %convolution_convert_fusion.1 = bf16[512,2048]{1,0:T(8,128)(2,1)} fusion(bf16[384,2048]{1,0:T(8,128)(2,1)S(1)} %copy-done, bf16[2048,384]{1,0:T(8,128)(2,1)} %param.35, f32[512,384]{1,0:T(8,128)S(1)} %fusion.66, f32[2048]{0:T(1024)S(1)} %copy-done.20, f32[512]{0:T(512)S(1)} %add_rsqrt_fusion.1, bf16[512,2048]{1,0:T(8,128)(2,1)} %all-gather.2.cloned.1.call-done, ...), kind=kOutput, calls=%fused_computation.23 | convolution fusion | flops 1619132416 | bytes 10233856 | tf_op jit(solution)/shard_map/dot_general | solution.py:248
  240.9 0.8 copy.48
  241.6 0.8 select_bitcast_fusion
  242.4 86.2 %all-reduce.5.cloned.1.call-done = bf16[512,2048]{1,0:T(8,128)(2,1)} async-done(((bf16[512,2048]{1,0:T(8,128)(2,1)}), bf16[512,2048]{1,0:T(8,128)(2,1)}) %all-reduce.5.cloned.1.call-update) | async-done | bytes 2097168 | tf_op jit(solution)/shard_map/psum | solution.py:247
  328.6 1.9 convert_add_fusion.1
  (74 shorter events, 1.3 us)
Async XLA Ops:
  7.2 227.2 %copy-start = (bf16[384,2048]{1,0:T(8,128)(2,1)S(1)}, bf16[384,2048]{1,0:T(8,128)(2,1)}, u32[]{:S(2)}) copy-start(bf16[384,2048]{1,0:T(8,128)(2,1)} %param.36) | copy-start | bytes 4718596
  7.2 78.2 %all-gather.2.cloned.1.call-start = ((), (), s32[]{:S(2)}) async-start(), calls=%async_computation.2 | async-start | bytes 2359296 | tf_op jit(solution)/shard_map/all_gather | solution.py:184
  11.1 5.8 %copy-start.15 = (s32[2]{0:T(128)S(1)}, s32[2]{0:T(128)}, u32[]{:S(2)}) copy-start(s32[2]{0:T(128)} %param.41) | copy-start | bytes 28
  11.1 5.9 %copy-start.12 = (s32[1,512]{1,0:T(1,128)S(1)}, s32[1,512]{1,0:T(1,128)}, u32[]{:S(2)}) copy-start(s32[1,512]{1,0:T(1,128)} %param.45) | copy-start | bytes 6148
  11.1 5.9 %copy-start.14 = (s32[2]{0:T(128)S(1)}, s32[2]{0:T(128)}, u32[]{:S(2)}) copy-start(s32[2]{0:T(128)} %param.43) | copy-start | bytes 28
  11.1 6.0 %copy-start.19 = (s32[2]{0:T(128)S(1)}, s32[2]{0:T(128)}, u32[]{:S(2)}) copy-start(s32[2]{0:T(128)} %param.42) | copy-start | bytes 28
  11.1 38.0 %all-to-all-start.1 = ((bf16[64,16,8,128]{3,1,0,2:T(8,128)(2,1)}), bf16[64,16,8,128]{3,1,0,2:T(8,128)(2,1)}, u32[]{:S(2)}, u32[]{:S(2)}) async-start(bf16[64,16,8,128]{3,1,0,2:T(8,128)(2,1)} %copy.39), calls=%async_computation.1 | async-start | bytes 4194304 | tf_op jit(solution)/shard_map/all_to_all | solution.py:214
  17.2 3.8 %copy-start.16 = (s32[2]{0:T(128)S(1)}, s32[2]{0:T(128)}, u32[]{:S(2)}) copy-start(s32[2]{0:T(128)} %param.44) | copy-start | bytes 28
  49.1 54.6 %all-to-all-start = ((bf16[64,16,8,128]{3,1,0,2:T(8,128)(2,1)}), bf16[64,16,8,128]{3,1,0,2:T(8,128)(2,1)}, u32[]{:S(2)}, u32[]{:S(2)}) async-start(bf16[64,16,8,128]{3,1,0,2:T(8,128)(2,1)} %copy.36), calls=%async_computation | async-start | bytes 4194304 | tf_op jit(solution)/shard_map/all_to_all | solution.py:213
  54.9 32.7 %copy-start.10 = (f32[2048]{0:T(1024)S(1)}, f32[2048]{0:T(1024)}, u32[]{:S(2)}) copy-start(f32[2048]{0:T(1024)} %param.25) | copy-start | bytes 24580
  54.9 171.7 %all-reduce.3.cloned.1.call-start = ((), (), s32[]{:S(2)}) async-start(), calls=%async_computation.3 | async-start | bytes 4194304 | tf_op jit(solution)/shard_map/psum | solution.py:242
  85.3 2.2 copy-start.2
  87.6 1.9 copy-start.11
  88.2 1.4 copy-start.1
  90.2 2.8 copy-start.17
  93.0 1.0 copy-start.8
  93.3 3.2 copy-start.18
  97.4 4.1 %copy-start.9 = (bf16[2048,128]{1,0:T(8,128)(2,1)S(1)}, bf16[2048,128]{1,0:T(8,128)(2,1)}, u32[]{:S(2)}) copy-start(bf16[2048,128]{1,0:T(8,128)(2,1)} %param.28) | copy-start | bytes 1572868
  107.8 4.9 %copy-start.13 = (bf16[2,4,1,128]{3,1,2,0:T(4,128)(2,1)S(1)}, bf16[2,4,1,128]{3,1,2,0:T(4,128)(2,1)}, u32[]{:S(2)}) copy-start(bf16[2,4,1,128]{3,1,2,0:T(4,128)(2,1)} %param.39) | copy-start | bytes 6148
  107.8 5.2 %copy-start.5 = (pred[2,256,4096]{1,2,0:T(8,128)(4,1)S(1)}, pred[2,256,4096]{1,2,0:T(8,128)(4,1)}, u32[]{:S(2)}) copy-start(pred[2,256,4096]{1,2,0:T(8,128)(4,1)} %or_and_fusion) | copy-start | bytes 6291460
  117.0 5.7 %copy-start.4 = (f32[2,4096,256,2]{2,1,3,0:T(8,128)}, f32[2,4096,256,2]{2,1,3,0:T(8,128)S(1)}, u32[]{:S(2)}) copy-start(f32[2,4096,256,2]{2,1,3,0:T(8,128)S(1)} %get-tuple-element.31) | copy-start | bytes 50331652
  122.8 9.8 %copy-start.21 = (bf16[2,4,1,128]{3,1,2,0:T(4,128)(2,1)S(1)}, bf16[2,4,1,128]{3,1,2,0:T(4,128)(2,1)}, u32[]{:S(2)}) copy-start(bf16[2,4,1,128]{3,1,2,0:T(4,128)(2,1)} %param.40) | copy-start | bytes 6148
  132.5 1.5 copy-start.7
  136.1 95.6 %copy-start.20 = (f32[2048]{0:T(1024)S(1)}, f32[2048]{0:T(1024)}, u32[]{:S(2)}) copy-start(f32[2048]{0:T(1024)} %param.33) | copy-start | bytes 24580
  136.1 192.5 %all-reduce.5.cloned.1.call-start = ((), (), s32[]{:S(2)}) async-start(), calls=%async_computation.4 | async-start | bytes 4194304 | tf_op jit(solution)/shard_map/psum | solution.py:247
  226.6 5.0 %copy-start.3 = (bf16[512,2048]{1,0:T(8,128)(2,1)S(1)}, bf16[512,2048]{1,0:T(8,128)(2,1)}, u32[]{:S(2)}) copy-start(bf16[512,2048]{1,0:T(8,128)(2,1)} %all-gather.2.cloned.1.call-done) | copy-start | bytes 6291460
  226.6 5.0 %copy-start.6 = (bf16[512,2048]{1,0:T(8,128)(2,1)S(1)}, bf16[512,2048]{1,0:T(8,128)(2,1)}, u32[]{:S(2)}) copy-start(bf16[512,2048]{1,0:T(8,128)(2,1)} %all-reduce.3.cloned.1.call-done) | copy-start | bytes 6291460
Sparse Core Ops, SparseCore 0:
  9.8 75.5 all-gather.1
  136.2 90.3 all-reduce.2
  241.0 87.5 all-reduce.4
where the time goes:
time: 338 us; the launch traced here: 337 us
  waiting for transfers between devices  230 us (68%)
  matrix products  34.5 us (10%)
  other arithmetic  26.8 us (8%)
  local copies, waits for them, and re-layouts  19.5 us (6%)
  between operations  14.2 us (4%)
  starting transfers between devices  11.9 us (4%)
    psum x1, waiting for transfers between devices, body(): lax.psum(jnp.dot(heads_out, w_out, preferred_element_type=jnp.float32).as...  90.3 us
    psum x1, waiting for transfers between devices, body(): lax.psum(jnp.dot(hidden, w_down, preferred_element_type=jnp.float32).asty...  86.2 us
    all_gather x1, waiting for transfers between devices, body(): all_rows = lax.all_gather(tokens, 'tp', axis=0, tiled=True)  30.4 us
    all_to_all x1, waiting for transfers between devices, body(): lax.all_to_all(pooled_values, 'tp', split_axis=2, concat_axis=0, tiled=True)  22.6 us
    dot_general x1, matrix products, attend_whole(): jnp.einsum('rckgw,rwkd->rckgd', window_weights.astype(jnp.bfloat16), wind...  9.68 us
    unnamed x48, local copies, waits for them, and re-layouts  9.65 us
    reduce_sum x2, other arithmetic, rms_rows(): mean_square = jnp.mean(values * values, axis=-1, keepdims=True)  7.22 us
  transfers between devices with their start and end apart: 5, of which 4 were waited for; matrix products, arithmetic and copies ran while one was open for 9% of the time, Pallas kernels for 0%

commit v1 on v0

--- a/solution.py
+++ b/solution.py
@@ -1,3 +1,4 @@
+import functools
 import math
 import jax
 import jax.numpy as jnp
@@ -9,6 +10,14 @@
 EPSILON = 1e-06
 ROPE_BASE = 1000000.0
 NEG_FILL = -1e30
+
+
+def push_columns_by_axis(piece_in, lane_axis):
+    known = lax.all_gather(piece_in, lane_axis).sum(axis=0)
+    return known
+
+
+try_all_group_over_axis = functools.partial(push_columns_by_axis, lane_axis="tp")
 
 
 def rms_rows(values, gain):
@@ -239,8 +248,8 @@
         .astype(jnp.bfloat16)
         .reshape(rows_total, heads_dev * head_dim)
     )
-    attn = lax.psum(
-        jnp.dot(heads_out, w_out, preferred_element_type=jnp.float32).astype(jnp.bfloat16), "tp"
+    attn = try_all_group_over_axis(
+        jnp.dot(heads_out, w_out, preferred_element_type=jnp.float32).astype(jnp.bfloat16)
     ).astype(jnp.float32)
     middle = residual + attn
     hidden = swiglu(rms_rows(middle, mlp_gain).astype(jnp.bfloat16), w_gate, w_up)

time: 338 us -> 431 us (1.28)
  waiting for transfers between devices: 230 us -> 315 us
  other arithmetic: 26.8 us -> 37.9 us
    all_gather x0 -> x1, waiting for transfers between devices: none -> 176 us  [push_columns_by_axis(): known = lax.all_gather(piece_in, lane_axis).sum(axis=0)]
    psum x1 -> x0, waiting for transfers between devices: 90.3 us -> none  [body(): lax.psum(jnp.dot(heads_out, w_out, preferred_element_type=jnp.float32).as...]
    reduce_sum x0 -> x1, other arithmetic: none -> 11 us  [push_columns_by_axis(): known = lax.all_gather(piece_in, lane_axis).sum(axis=0)]
    unnamed x48 -> x50, local copies, waits for them, and re-layouts: 9.65 us -> 9.64 us
  transfers between devices with their start and end apart: 5 -> 5, of which waited for: 4 -> 4; matrix products, arithmetic and copies ran while one was open for 9% -> 7% of each run, Pallas kernels for 0% -> 0%
where the time goes in v1:
time: 431 us
  waiting for transfers between devices  315 us (73%)
  other arithmetic  37.9 us (9%)
  matrix products  33 us (8%)
  local copies, waits for them, and re-layouts  19.5 us (5%)
  between operations  14.2 us (3%)
  starting transfers between devices  11.6 us (3%)
    all_gather x1, waiting for transfers between devices, push_columns_by_axis(): known = lax.all_gather(piece_in, lane_axis).sum(axis=0)  176 us
    psum x1, waiting for transfers between devices, body(): lax.psum(jnp.dot(hidden, w_down, preferred_element_type=jnp.float32).asty...  84.6 us
    all_gather x1, waiting for transfers between devices, body(): all_rows = lax.all_gather(tokens, 'tp', axis=0, tiled=True)  30.4 us
    all_to_all x1, waiting for transfers between devices, body(): lax.all_to_all(pooled_values, 'tp', split_axis=2, concat_axis=0, tiled=True)  22.6 us
    reduce_sum x1, other arithmetic, push_columns_by_axis(): known = lax.all_gather(piece_in, lane_axis).sum(axis=0)  11 us
    dot_general x1, matrix products, attend_whole(): jnp.einsum('rckgw,rwkd->rckgd', window_weights.astype(jnp.bfloat16), wind...  9.67 us
    unnamed x50, local copies, waits for them, and re-layouts  9.64 us
  transfers between devices with their start and end apart: 5, of which 4 were waited for; matrix products, arithmetic and copies ran while one was open for 7% of the time, Pallas kernels for 0%

profile of v1, /device:TPU:8, one launch (start us, length us, event | category | flops | bytes accessed | tf_op | source)
XLA Modules:
  0.0 430.8 jit_solution(2428506700778408653)
XLA Ops:
  7.2 0.7 all-gather.4.cloned.1.call-update
  7.9 3.2 copy.39
  11.1 5.8 %all-to-all-start.1 = ((bf16[64,16,8,128]{3,1,0,2:T(8,128)(2,1)}), bf16[64,16,8,128]{3,1,0,2:T(8,128)(2,1)}, u32[]{:S(2)}, u32[]{:S(2)}) async-start(bf16[64,16,8,128]{3,1,0,2:T(8,128)(2,1)} %copy.39), calls=%async_computation.1 | async-start | bytes 4194304 | tf_op jit(solution)/shard_map/all_to_all | solution.py:223
  17.2 3.2 copy.36
  20.5 0.5 multiply_cosine_fusion.1
  21.0 0.2 or_and_fusion.1
  21.3 0.6 iota_add_fusion
  22.0 4.6 %or_and_fusion = pred[2,256,4096]{1,2,0:T(8,128)(4,1)} fusion(s32[256,4096]{0,1:T(8,128)S(1)} %iota_add_fusion, s32[2]{0:T(128)S(1)} %copy-done.16, pred[2,4096]{1,0:T(4,128)(4,1)S(1)} %get-tuple-element.21, pred[2,4096]{1,0:T(4,128)(4,1)S(1)} %get-tuple-element.20), kind=kLoop, calls=%fused_computation.12 | loop fusion | flops 6291456 | bytes 6307848 | tf_op jit(solution)/shard_map/and | solution.py:111
  26.6 22.6 %all-to-all-done.1 = bf16[64,16,8,128]{3,1,0,2:T(8,128)(2,1)} async-done(((bf16[64,16,8,128]{3,1,0,2:T(8,128)(2,1)}), bf16[64,16,8,128]{3,1,0,2:T(8,128)(2,1)}, u32[]{:S(2)}, u32[]{:S(2)}) %all-to-all-start.1) | async-done | bytes 2097184 | tf_op jit(solution)/shard_map/all_to_all | solution.py:223
  49.1 5.7 %all-to-all-start = ((bf16[64,16,8,128]{3,1,0,2:T(8,128)(2,1)}), bf16[64,16,8,128]{3,1,0,2:T(8,128)(2,1)}, u32[]{:S(2)}, u32[]{:S(2)}) async-start(bf16[64,16,8,128]{3,1,0,2:T(8,128)(2,1)} %copy.36), calls=%async_computation | async-start | bytes 4194304 | tf_op jit(solution)/shard_map/all_to_all | solution.py:222
  54.9 30.4 %all-gather.4.cloned.1.call-done = bf16[512,2048]{1,0:T(8,128)(2,1)} async-done(((bf16[64,2048]{1,0:T(8,128)(2,1)}), bf16[512,2048]{1,0:T(8,128)(2,1)}) %all-gather.4.cloned.1.call-update) | async-done | bytes 2097168 | tf_op jit(solution)/shard_map/all_gather | solution.py:193
  85.3 2.2 fusion.9
  87.6 0.5 fusion.11
  88.2 1.4 copy-done.1
  89.5 0.7 fusion.20
  90.2 0.1 copy.47
  90.4 2.6 multiply_reduce_fusion.1
  93.3 0.2 copy.35
  93.5 0.2 copy.34
  93.7 0.3 copy-done.8
  94.0 2.4 multiply_reduce_fusion.2
  96.6 0.6 fusion.44
  97.3 0.1 copy.59
  97.4 4.0 gather_fusion.1
  101.5 2.3 convolution_convert_fusion.2
  103.8 4.0 gather_fusion
  107.7 4.9 %bitcast_select_fusion.1 = (bf16[512,16,1,128]{3,1,0,2:T(8,128)(2,1)}, bf16[512,16,1,128]{3,1,0,2:T(8,128)(2,1)}) fusion(bf16[512,16,128]{2,1,0:T(8,128)(2,1)} %gather_fusion.1, pred[512]{0:T(512)(128)(4,1)S(1)} %compare_and_fusion, bf16[512,16,128]{2,1,0:T(8,128)(2,1)} %gather_fusion), kind=kLoop, calls=%fused_computation.24 | loop fusion | flops 2097152 | bytes 8389120 | tf_op jit(solution)/shard_map/jit(_take)/select_n | solution.py:228
  112.6 0.3 select_reduce_fusion.1
  112.9 4.1 fusion
  117.0 0.4 select_reduce_fusion
  117.4 0.2 fusion.23
  117.7 0.4 fusion.31
  118.1 3.9 fusion.3
  122.0 0.7 copy-done.4
  122.7 9.7 %fusion.6 = f32[2,128,256,2]{1,2,3,0:T(8,128)S(1)} fusion(bf16[2,4096,128,1]{2,1,3,0:T(8,128)(2,1)} %bitcast.161, f32[2,4096,256,2]{2,1,3,0:T(8,128)} %copy-done.4, f32[2,256,2]{1,2,0:T(2,128)S(1)} %maximum_maximum_fusion, pred[2,256,4096]{1,2,0:T(8,128)(4,1)} %or_and_fusion), kind=kOutput, calls=%fused_computation.10 | convolution fusion | flops 1090519040 | bytes 21499904 | tf_op jit(solution)/shard_map/rckgw,rwkd->rckgd/dot_general | solution.py:144
  132.5 0.4 fusion.22
  132.9 0.4 copy.46
  133.3 0.6 mul.265
  134.0 2.0 convolution_convert_fusion
  136.1 176.2 %all-gather.6.cloned.1.call-done = bf16[4096,2048]{1,0:T(8,128)(2,1)} async-done(((bf16[512,2048]{1,0:T(8,128)(2,1)}), bf16[4096,2048]{1,0:T(8,128)(2,1)}) %all-gather.6.cloned.1.call-update) | async-done | bytes 16777232 | tf_op jit(solution)/shard_map/all_gather | solution.py:16
  312.3 11.0 %reduce_sum.81 = bf16[512,2048]{1,0:T(8,128)(2,1)} reduce(bf16[8,512,2048]{2,1,0:T(8,128)(2,1)} %bitcast.160, bf16[]{:T(256)} %constant.38.clone.1), dimensions={0}, to_apply=%region_9.11 | reduce | flops 7340032 | bytes 18874370 | tf_op jit(solution)/shard_map/reduce_sum | solution.py:16
  323.3 5.0 %multiply_reduce_fusion = (f32[512]{0:T(512)S(1)}, f32[512,2048]{1,0:T(8,128)}) fusion(bf16[512,2048]{1,0:T(8,128)(2,1)} %reduce_sum.81, bf16[512,2048]{1,0:T(8,128)(2,1)} %all-gather.4.cloned.1.call-done), kind=kLoop, calls=%fused_computation.20 | loop fusion | flops 5242368 | bytes 8390656 | tf_op jit(solution)/shard_map/reduce_sum | solution.py:24
  328.3 1.3 fusion.66
  329.6 6.4 %convolution_convert_fusion.1 = bf16[512,2048]{1,0:T(8,128)(2,1)} fusion(bf16[384,2048]{1,0:T(8,128)(2,1)S(1)} %copy-done, bf16[2048,384]{1,0:T(8,128)(2,1)} %param.35, f32[512,384]{1,0:T(8,128)S(1)} %fusion.66, f32[2048]{0:T(1024)S(1)} %copy-done.21, f32[512]{0:T(512)S(1)} %add_rsqrt_fusion.1, bf16[512,2048]{1,0:T(8,128)(2,1)} %all-gather.4.cloned.1.call-done, ...), kind=kOutput, calls=%fused_computation.23 | convolution fusion | flops 1619132416 | bytes 10233856 | tf_op jit(solution)/shard_map/dot_general | solution.py:257
  336.1 0.8 copy.48
  336.9 0.8 select_bitcast_fusion
  337.6 84.6 %all-reduce.2.cloned.1.call-done = bf16[512,2048]{1,0:T(8,128)(2,1)} async-done(((bf16[512,2048]{1,0:T(8,128)(2,1)}), bf16[512,2048]{1,0:T(8,128)(2,1)}) %all-reduce.2.cloned.1.call-update) | async-done | bytes 2097168 | tf_op jit(solution)/shard_map/psum | solution.py:256
  422.3 1.9 convert_add_fusion.1
  (77 shorter events, 1.3 us)
Async XLA Ops:
  7.2 322.4 %copy-start = (bf16[384,2048]{1,0:T(8,128)(2,1)S(1)}, bf16[384,2048]{1,0:T(8,128)(2,1)}, u32[]{:S(2)}) copy-start(bf16[384,2048]{1,0:T(8,128)(2,1)} %param.36) | copy-start | bytes 4718596
  7.2 78.2 %all-gather.4.cloned.1.call-start = ((), (), s32[]{:S(2)}) async-start(), calls=%async_computation.2 | async-start | bytes 2359296 | tf_op jit(solution)/shard_map/all_gather | solution.py:193
  11.1 5.8 %copy-start.15 = (s32[2]{0:T(128)S(1)}, s32[2]{0:T(128)}, u32[]{:S(2)}) copy-start(s32[2]{0:T(128)} %param.41) | copy-start | bytes 28
  11.1 5.9 %copy-start.12 = (s32[1,512]{1,0:T(1,128)S(1)}, s32[1,512]{1,0:T(1,128)}, u32[]{:S(2)}) copy-start(s32[1,512]{1,0:T(1,128)} %param.45) | copy-start | bytes 6148
  11.1 5.9 %copy-start.14 = (s32[2]{0:T(128)S(1)}, s32[2]{0:T(128)}, u32[]{:S(2)}) copy-start(s32[2]{0:T(128)} %param.43) | copy-start | bytes 28
  11.1 6.0 %copy-start.19 = (s32[2]{0:T(128)S(1)}, s32[2]{0:T(128)}, u32[]{:S(2)}) copy-start(s32[2]{0:T(128)} %param.42) | copy-start | bytes 28
  11.1 38.0 %all-to-all-start.1 = ((bf16[64,16,8,128]{3,1,0,2:T(8,128)(2,1)}), bf16[64,16,8,128]{3,1,0,2:T(8,128)(2,1)}, u32[]{:S(2)}, u32[]{:S(2)}) async-start(bf16[64,16,8,128]{3,1,0,2:T(8,128)(2,1)} %copy.39), calls=%async_computation.1 | async-start | bytes 4194304 | tf_op jit(solution)/shard_map/all_to_all | solution.py:223
  17.2 3.8 copy-start.16
  49.1 54.6 %all-to-all-start = ((bf16[64,16,8,128]{3,1,0,2:T(8,128)(2,1)}), bf16[64,16,8,128]{3,1,0,2:T(8,128)(2,1)}, u32[]{:S(2)}, u32[]{:S(2)}) async-start(bf16[64,16,8,128]{3,1,0,2:T(8,128)(2,1)} %copy.36), calls=%async_computation | async-start | bytes 4194304 | tf_op jit(solution)/shard_map/all_to_all | solution.py:222
  54.9 32.7 %copy-start.10 = (f32[2048]{0:T(1024)S(1)}, f32[2048]{0:T(1024)}, u32[]{:S(2)}) copy-start(f32[2048]{0:T(1024)} %param.25) | copy-start | bytes 24580
  54.9 257.4 %all-gather.6.cloned.1.call-start = ((), (), s32[]{:S(2)}) async-start(), calls=%async_computation.4 | async-start | bytes 18874368 | tf_op jit(solution)/shard_map/all_gather | solution.py:16
  85.3 2.2 copy-start.2
  87.6 1.9 copy-start.11
  88.1 1.4 copy-start.1
  90.2 2.8 copy-start.17
  93.0 1.0 copy-start.8
  93.2 3.2 copy-start.18
  97.4 4.0 copy-start.9
  107.7 4.9 %copy-start.13 = (bf16[2,4,1,128]{3,1,2,0:T(4,128)(2,1)S(1)}, bf16[2,4,1,128]{3,1,2,0:T(4,128)(2,1)}, u32[]{:S(2)}) copy-start(bf16[2,4,1,128]{3,1,2,0:T(4,128)(2,1)} %param.39) | copy-start | bytes 6148
  107.7 5.2 %copy-start.5 = (pred[2,256,4096]{1,2,0:T(8,128)(4,1)S(1)}, pred[2,256,4096]{1,2,0:T(8,128)(4,1)}, u32[]{:S(2)}) copy-start(pred[2,256,4096]{1,2,0:T(8,128)(4,1)} %or_and_fusion) | copy-start | bytes 6291460
  117.0 5.7 %copy-start.4 = (f32[2,4096,256,2]{2,1,3,0:T(8,128)}, f32[2,4096,256,2]{2,1,3,0:T(8,128)S(1)}, u32[]{:S(2)}) copy-start(f32[2,4096,256,2]{2,1,3,0:T(8,128)S(1)} %get-tuple-element.31) | copy-start | bytes 50331652
  122.7 9.8 %copy-start.22 = (bf16[2,4,1,128]{3,1,2,0:T(4,128)(2,1)S(1)}, bf16[2,4,1,128]{3,1,2,0:T(4,128)(2,1)}, u32[]{:S(2)}) copy-start(bf16[2,4,1,128]{3,1,2,0:T(4,128)(2,1)} %param.40) | copy-start | bytes 6148
  132.4 1.5 copy-start.7
  136.0 286.3 %all-reduce.2.cloned.1.call-start = ((), (), s32[]{:S(2)}) async-start(), calls=%async_computation.3 | async-start | bytes 4194304 | tf_op jit(solution)/shard_map/psum | solution.py:256
  323.3 5.0 %copy-start.3 = (bf16[512,2048]{1,0:T(8,128)(2,1)S(1)}, bf16[512,2048]{1,0:T(8,128)(2,1)}, u32[]{:S(2)}) copy-start(bf16[512,2048]{1,0:T(8,128)(2,1)} %all-gather.4.cloned.1.call-done) | copy-start | bytes 6291460
  323.3 5.0 %copy-start.6 = (bf16[512,2048]{1,0:T(8,128)(2,1)S(1)}, bf16[512,2048]{1,0:T(8,128)(2,1)}, u32[]{:S(2)}) copy-start(bf16[512,2048]{1,0:T(8,128)(2,1)} %reduce_sum.81) | copy-start | bytes 6291460
  323.3 5.0 %copy-start.20 = (bf16[2048,384]{1,0:T(8,128)(2,1)S(1)}, bf16[2048,384]{1,0:T(8,128)(2,1)}, u32[]{:S(2)}) copy-start(bf16[2048,384]{1,0:T(8,128)(2,1)} %param.34) | copy-start | bytes 4718596
  323.3 5.0 %copy-start.21 = (f32[2048]{0:T(1024)S(1)}, f32[2048]{0:T(1024)}, u32[]{:S(2)}) copy-start(f32[2048]{0:T(1024)} %param.33) | copy-start | bytes 24580
Sparse Core Ops, SparseCore 0:
  9.8 75.5 all-gather.3
  136.1 176.0 all-gather.5
  336.2 86.0 all-reduce.1
